TPU v7x, 128 devices: a whole 4x4x4 slice. The times are simulated.
128 devices in a mesh: room: 4 (over x_hi, core), geom: 32 (over z, x_lo, y).
Axes of the slice: x: 4 (x_hi: 2, x_lo: 2; x = x_hi * 2 + x_lo), y: 4, z: 4, core: 2. Of those that a mesh axis runs over, the one named last changes fastest.
Arguments:
- queries: bfloat16 [4, 4096, 512], P('room', 'geom'), may hold values from -6 to 6
- features: bfloat16 [4, 4096, 512], P('room', 'geom'), may hold values from -45 to 45
- visible: int32 [4, 32, 32], P('room', 'geom'), may hold values from 0 to 1, as said below
- cotangent: bfloat16 [4, 4096, 512], P('room', 'geom'), may hold values from -0.125 to 0.125
- w_query: bfloat16 [512, 512], replicated, may hold values from -0.25 to 0.25
- w_key: bfloat16 [512, 512], replicated, may hold values from -0.25 to 0.25
- w_value: bfloat16 [512, 512], replicated, may hold values from -0.25 to 0.25
- w_out: bfloat16 [512, 512], replicated, may hold values from -0.25 to 0.25
- w_up: bfloat16 [512, 1024], replicated, may hold values from -0.25 to 0.25
- w_down: bfloat16 [1024, 512], replicated, may hold values from -0.1875 to 0.1875
- gain_attn: float32 [512], replicated, may hold values from 0.25 to 1.75
- gain_mlp: float32 [512], replicated, may hold values from 0.25 to 1.75
Outputs:
- output: bfloat16 [4, 4096, 512], P('room', 'geom')
- grad_query_w: bfloat16 [512, 512], replicated
- grad_key_w: bfloat16 [512, 512], replicated
- grad_value_w: bfloat16 [512, 512], replicated
- grad_out_w: bfloat16 [512, 512], replicated
- grad_up_w: bfloat16 [512, 1024], replicated
- grad_down_w: bfloat16 [1024, 512], replicated
- grad_gain_attn: bfloat16 [512], replicated
- grad_gain_mlp: bfloat16 [512], replicated
Inputs may be any that keep to these rules, and one draw needn't show every extreme that they name: `visible`: every query block sees at least one key block.
All inputs are finite; a program needn't handle non-finite values.
Results may differ from a plain program's by a relative error of at most 0.017.
The roundings to bfloat16 on the way count: a program that leaves them out, or rounds other values in their place, can miss the bound.
Values may be sent and summed in bfloat16 or wider, within the bound.
No kernel may reach another device: no remote copies, remote signals or barrier semaphores. Data moves between devices by JAX's collectives and lax.ppermute only.
A program may use at most 128 MiB of HBM per device.

v0:
```python
import math
import jax
import jax.numpy as jnp
from jax import lax
from jax.sharding import PartitionSpec as P

HEADS = 4
BLK = 128
EPSILON = 1e-05
GELU_COEF = math.sqrt(2.0 / math.pi)


def normalize(inputs, gain):
    center = inputs - jnp.mean(inputs, axis=-1, keepdims=True)
    inverse = lax.rsqrt(jnp.mean(center * center, axis=-1, keepdims=True) + EPSILON)
    scaled = center * inverse
    return (scaled, inverse, scaled * gain)


def gelu_pair(inputs):
    inner = GELU_COEF * (inputs + 0.044715 * inputs * inputs * inputs)
    tangent = jnp.tanh(inner)
    value = 0.5 * inputs * (1.0 + tangent)
    slope = 0.5 * (1.0 + tangent) + 0.5 * inputs * (1.0 - tangent * tangent) * GELU_COEF * (
        1.0 + 3.0 * 0.044715 * inputs * inputs
    )
    return (value, slope)


def mult_nt(left, right):
    return lax.dot_general(
        left, right, (((1,), (1,)), ((), ())), preferred_element_type=jnp.float32
    )


def mult_tn(left, right):
    return lax.dot_general(
        left, right, (((0,), (0,)), ((), ())), preferred_element_type=jnp.float32
    )


def device_step(
    queries,
    visible,
    cotangent,
    key_rows,
    value_rows,
    w_query,
    w_out,
    w_up,
    w_down,
    gain_attn,
    gain_mlp,
):
    head_size = key_rows.shape[1] // HEADS
    factor = 1.0 / math.sqrt(head_size)
    allowed = jnp.repeat(jnp.repeat(visible > 0, BLK, axis=0), BLK, axis=1)
    inputs = queries.astype(jnp.float32)
    scaled_one, inverse_one, normed = normalize(inputs, gain_attn)
    normed_b = normed.astype(jnp.bfloat16)
    query_rows = jnp.dot(normed_b, w_query, preferred_element_type=jnp.float32).astype(jnp.bfloat16)
    contexts = []
    saved = []
    for head_index in range(HEADS):
        lower = head_index * head_size
        query_head = query_rows[:, lower : lower + head_size]
        key_head = key_rows[:, lower : lower + head_size]
        value_head = value_rows[:, lower : lower + head_size]
        scores = mult_nt(query_head, key_head) * factor
        scores = jnp.where(allowed, scores, -1e30)
        highest = jnp.max(scores, axis=-1, keepdims=True)
        expo = jnp.exp(scores - highest)
        attend = expo / jnp.sum(expo, axis=-1, keepdims=True)
        attend_b = attend.astype(jnp.bfloat16)
        contexts.append(
            jnp.dot(attend_b, value_head, preferred_element_type=jnp.float32).astype(jnp.bfloat16)
        )
        saved.append((attend, attend_b))
    context = jnp.concatenate(contexts, axis=1)
    mixed = inputs + jnp.dot(context, w_out, preferred_element_type=jnp.float32)
    scaled_two, inverse_two, normed_two = normalize(mixed, gain_mlp)
    normed_two_b = normed_two.astype(jnp.bfloat16)
    upper = jnp.dot(normed_two_b, w_up, preferred_element_type=jnp.float32)
    activated, slope = gelu_pair(upper)
    activated_b = activated.astype(jnp.bfloat16)
    output = (mixed + jnp.dot(activated_b, w_down, preferred_element_type=jnp.float32)).astype(
        jnp.bfloat16
    )
    grad_down = mult_tn(activated_b, cotangent)
    grad_activated = mult_nt(cotangent, w_down)
    grad_upper_b = (grad_activated * slope).astype(jnp.bfloat16)
    grad_up = mult_tn(normed_two_b, grad_upper_b)
    grad_normed_two = mult_nt(grad_upper_b, w_up)
    grad_gain_mlp = jnp.sum(grad_normed_two * scaled_two, axis=0)
    grad_scaled = grad_normed_two * gain_mlp
    mean_one = jnp.mean(grad_scaled, axis=-1, keepdims=True)
    mean_two = jnp.mean(grad_scaled * scaled_two, axis=-1, keepdims=True)
    grad_mixed = cotangent.astype(jnp.float32) + inverse_two * (
        grad_scaled - mean_one - scaled_two * mean_two
    )
    grad_mixed_b = grad_mixed.astype(jnp.bfloat16)
    grad_out = mult_tn(context, grad_mixed_b)
    grad_context = mult_nt(grad_mixed_b, w_out).astype(jnp.bfloat16)
    grad_queries = []
    grad_keys = []
    grad_values = []
    for head_index in range(HEADS):
        lower = head_index * head_size
        query_head = query_rows[:, lower : lower + head_size]
        key_head = key_rows[:, lower : lower + head_size]
        value_head = value_rows[:, lower : lower + head_size]
        attend, attend_b = saved[head_index]
        grad_head = grad_context[:, lower : lower + head_size]
        grad_attend = mult_nt(grad_head, value_head)
        grad_values.append(mult_tn(attend_b, grad_head))
        centre = jnp.sum(attend * grad_attend, axis=-1, keepdims=True)
        grad_scores = (attend * (grad_attend - centre) * factor).astype(jnp.bfloat16)
        grad_queries.append(jnp.dot(grad_scores, key_head, preferred_element_type=jnp.float32))
        grad_keys.append(mult_tn(grad_scores, query_head))
    grad_query_rows = jnp.concatenate(grad_queries, axis=1).astype(jnp.bfloat16)
    partial_keys = jnp.concatenate(grad_keys, axis=1).astype(jnp.bfloat16)
    partial_values = jnp.concatenate(grad_values, axis=1).astype(jnp.bfloat16)
    grad_query = mult_tn(normed_b, grad_query_rows)
    grad_normed = mult_nt(grad_query_rows, w_query)
    grad_gain_attn = jnp.sum(grad_normed * scaled_one, axis=0)
    grads = (grad_query, grad_out, grad_up, grad_down, grad_gain_attn, grad_gain_mlp)
    return (output, grads, partial_keys, partial_values)


def local(
    queries,
    features,
    visible,
    cotangent,
    w_query,
    w_key,
    w_value,
    w_out,
    w_up,
    w_down,
    gain_attn,
    gain_mlp,
):
    local_feat = features[0]
    local_keys = jnp.dot(local_feat, w_key, preferred_element_type=jnp.float32).astype(jnp.bfloat16)
    local_values = jnp.dot(local_feat, w_value, preferred_element_type=jnp.float32).astype(
        jnp.bfloat16
    )
    key_rows, value_rows = (
        lax.all_gather(local_keys, "geom", axis=0, tiled=True),
        lax.all_gather(local_values, "geom", axis=0, tiled=True),
    )
    output, grads, partial_keys, partial_values = device_step(
        queries[0],
        visible[0],
        cotangent[0],
        key_rows,
        value_rows,
        w_query,
        w_out,
        w_up,
        w_down,
        gain_attn,
        gain_mlp,
    )
    key_sum, value_sum = (
        lax.psum_scatter(partial_keys.astype(jnp.float32), "geom", scatter_dimension=0, tiled=True),
        lax.psum_scatter(
            partial_values.astype(jnp.float32), "geom", scatter_dimension=0, tiled=True
        ),
    )
    feat_float = local_feat.astype(jnp.float32)
    grad_key = lax.dot_general(
        feat_float,
        key_sum,
        (((0,), (0,)), ((), ())),
        precision=lax.Precision.HIGHEST,
        preferred_element_type=jnp.float32,
    )
    grad_value = lax.dot_general(
        feat_float,
        value_sum,
        (((0,), (0,)), ((), ())),
        precision=lax.Precision.HIGHEST,
        preferred_element_type=jnp.float32,
    )
    grad_query, grad_out, grad_up, grad_down, grad_gain_attn, grad_gain_mlp = grads
    totals = lax.psum(
        (
            grad_query,
            grad_key,
            grad_value,
            grad_out,
            grad_up,
            grad_down,
            grad_gain_attn,
            grad_gain_mlp,
        ),
        ("room", "geom"),
    )
    summed = [piece.astype(jnp.bfloat16) for piece in totals]
    return (
        output[None],
        summed[0],
        summed[1],
        summed[2],
        summed[3],
        summed[4],
        summed[5],
        summed[6],
        summed[7],
    )


def solution(mesh):
    placed = (
        P("room", "geom", None),
        P("room", "geom", None),
        P("room", "geom", None),
        P("room", "geom", None),
        P(),
        P(),
        P(),
        P(),
        P(),
        P(),
        P(),
        P(),
    )
    return jax.shard_map(
        local,
        mesh=mesh,
        in_specs=placed,
        out_specs=(P("room", "geom", None), P(), P(), P(), P(), P(), P(), P(), P()),
        check_vma=False,
    )
```

profile of v0, /device:TPU:0, one launch (start us, length us, event | category | flops | bytes accessed | tf_op | source)
XLA Modules:
  0.0 832.1 jit_solution(216690923784676051)
XLA Ops:
  7.3 2.1 convolution_convert_fusion.10
  9.5 2.0 convolution_convert_fusion.9
  11.5 1.0 convert_reduce_fusion
  12.6 1.1 fusion.54
  14.1 156.3 %all-gather.3.cloned.1.call-done = bf16[4096,512]{1,0:T(8,128)(2,1)} async-done(((bf16[128,512]{1,0:T(8,128)(2,1)}), bf16[4096,512]{1,0:T(8,128)(2,1)}) %all-gather.3.cloned.1.call-update) | async-done | bytes 4194320 | tf_op jit(solution)/shard_map/all_gather | solution.py:150
  170.4 1.9 fusion.99
  172.3 1.4 copy-done.8
  173.7 0.4 fusion.5
  174.2 0.6 fusion.98
  174.7 1.3 copy-done.5
  176.0 0.4 fusion.7
  176.4 0.5 fusion.97
  177.0 0.4 fusion.9
  177.5 0.5 fusion.96
  178.3 0.4 fusion.11
  178.8 151.2 %all-gather.5.cloned.1.call-done = bf16[4096,512]{1,0:T(8,128)(2,1)} async-done(((bf16[128,512]{1,0:T(8,128)(2,1)}), bf16[4096,512]{1,0:T(8,128)(2,1)}) %all-gather.5.cloned.1.call-update) | async-done | bytes 4194320 | tf_op jit(solution)/shard_map/all_gather | solution.py:151
  329.9 2.7 convolution_convert_fusion.19
  332.7 1.0 copy-done.78
  333.7 0.7 convolution_convert_fusion.18
  334.5 0.8 copy-done.3
  335.3 0.7 convolution_convert_fusion.17
  336.1 0.7 convolution_convert_fusion.16
  338.5 0.6 fusion.12
  339.1 1.1 multiply_reduce_fusion.4
  340.7 0.6 convolution_convert_fusion.2
  341.4 1.0 copy-done.9
  342.4 0.6 convolution_convert_fusion.3
  343.0 0.6 convolution_convert_fusion.1
  343.7 0.6 convolution_convert_fusion
  344.3 3.6 maximum_convert_fusion.1
  348.6 2.7 multiply_reduce_fusion.3
  351.3 0.7 multiply_convert_fusion.3
  352.2 0.5 convolution_convert_fusion.7
  352.7 0.9 copy-done.79
  353.7 0.9 copy-done.7
  354.5 0.7 multiply_reduce_fusion.2
  355.2 0.7 multiply_convert_fusion.2
  356.0 0.5 convolution_convert_fusion.6
  356.4 1.5 copy-done.4
  357.9 0.7 multiply_reduce_fusion.1
  358.6 0.7 multiply_convert_fusion.1
  359.4 0.5 convolution_convert_fusion.5
  360.1 0.7 multiply_reduce_fusion
  360.8 0.7 multiply_convert_fusion
  361.5 1.0 copy-done.17
  362.4 0.5 convolution_convert_fusion.4
  362.9 3.9 maximum_convert_fusion
  366.8 1.9 convolution_convert_fusion.15
  368.8 2.1 convolution_convert_fusion.14
  370.9 0.6 convolution_convert_fusion.13
  371.5 0.6 convolution_convert_fusion.12
  372.1 0.9 fusion.14
  373.0 0.5 fusion.86
  373.6 1.3 fusion.79
  374.9 1.4 fusion.78
  376.3 1.9 fusion.55
  378.1 1.0 fusion.15
  379.2 147.8 %reduce-scatter.5.cloned.1.call-done = f32[128,512]{1,0:T(8,128)} async-done(((f32[4096,512]{1,0:T(8,128)}), f32[128,512]{1,0:T(8,128)}) %reduce-scatter.5.cloned.1.call-update) | async-done | bytes 262160 | tf_op jit(solution)/shard_map/reduce_scatter | solution.py:168
  526.9 2.5 convolution_bitcast_fusion
  529.5 174.9 %reduce-scatter.3.cloned.1.call-done = f32[128,512]{1,0:T(8,128)} async-done(((f32[4096,512]{1,0:T(8,128)}), f32[128,512]{1,0:T(8,128)}) %reduce-scatter.3.cloned.1.call-update) | async-done | bytes 262160 | tf_op jit(solution)/shard_map/reduce_scatter | solution.py:167
  704.4 2.6 convolution_bitcast_fusion.1
  707.0 114.5 %all-reduce.2 = (bf16[512,512]{1,0:T(8,128)(2,1)}, bf16[512,512]{0,1:T(8,128)(2,1)}, bf16[512,512]{0,1:T(8,128)(2,1)}, bf16[512,512]{1,0:T(8,128)(2,1)}, bf16[51...) all-reduce(f32[512,512]{1,0:T(8,128)} %fusion.78, ...), channel_id=1, replica_groups=mesh['room'=4,'geom'=32] {'room','geom'}, use_global_device_ids=true, to_apply=%region_18.19 | all-reduce | flops 2098176 | bytes 12589056 | tf_op jit(solution)/shard_map/psum | solution.py:188
  821.4 2.0 copy.21
  823.5 2.0 copy.22
  (178 shorter events, 4.3 us)
Async XLA Ops:
  7.2 330.5 %copy-start = (bf16[512,1024]{1,0:T(8,128)(2,1)S(1)}, bf16[512,1024]{1,0:T(8,128)(2,1)}, u32[]{:S(2)}) copy-start(bf16[512,1024]{1,0:T(8,128)(2,1)} %param.20) | copy-start | bytes 3145732
  7.2 6.6 copy-start.19
  7.2 6.5 copy-start.82
  7.2 6.6 copy-start.30
  7.2 6.6 copy-start.45
  7.2 163.2 %all-gather.3.cloned.1.call-start = ((), (), s32[]{:S(2)}) async-start(), calls=%async_computation.2 | async-start | bytes 4325376 | tf_op jit(solution)/shard_map/all_gather | solution.py:150
  9.4 320.5 %all-gather.5.cloned.1.call-start = ((), (), s32[]{:S(2)}) async-start(), calls=%async_computation.3 | async-start | bytes 4325376 | tf_op jit(solution)/shard_map/all_gather | solution.py:151
  11.5 515.4 %reduce-scatter.5.cloned.1.call-start = ((), (), s32[]{:S(2)}) async-start(), calls=%async_computation.5 | async-start | bytes 8650752 | tf_op jit(solution)/shard_map/reduce_scatter | solution.py:168
  12.6 161.6 %copy-start.47 = (f32[128]{0:T(128)}, f32[128]{0:T(128)S(1)}, u32[]{:S(2)}) copy-start(f32[128]{0:T(128)S(1)} %broadcast_multiply_fusion.3) | copy-start | bytes 1540
  13.7 160.4 %copy-start.62 = (f32[128]{0:T(128)}, f32[128]{0:T(128)S(1)}, u32[]{:S(2)}) copy-start(f32[128]{0:T(128)S(1)} %add_rsqrt_fusion.1) | copy-start | bytes 1540
  14.1 163.4 %copy-start.24 = (bf16[128,512]{1,0:T(8,128)(2,1)}, bf16[128,512]{1,0:T(8,128)(2,1)S(1)}, u32[]{:S(2)}) copy-start(bf16[128,512]{1,0:T(8,128)(2,1)S(1)} %convolution_convert_fusion.11) | copy-start | bytes 393220
  170.4 3.7 copy-start.11
  172.3 157.6 %copy-start.58 = (f32[128]{0:T(128)}, f32[128]{0:T(128)S(1)}, u32[]{:S(2)}) copy-start(f32[128]{0:T(128)S(1)} %get-tuple-element.35) | copy-start | bytes 1540
  174.1 155.8 %copy-start.73 = (f32[128]{0:T(128)}, f32[128]{0:T(128)S(1)}, u32[]{:S(2)}) copy-start(f32[128]{0:T(128)S(1)} %fusion.5) | copy-start | bytes 1540
  174.7 157.9 %copy-start.55 = (f32[128]{0:T(128)}, f32[128]{0:T(128)S(1)}, u32[]{:S(2)}) copy-start(f32[128]{0:T(128)S(1)} %get-tuple-element.33) | copy-start | bytes 1540
  176.4 156.2 %copy-start.70 = (f32[128]{0:T(128)}, f32[128]{0:T(128)S(1)}, u32[]{:S(2)}) copy-start(f32[128]{0:T(128)S(1)} %fusion.7) | copy-start | bytes 1540
  177.0 157.5 %copy-start.52 = (f32[128]{0:T(128)}, f32[128]{0:T(128)S(1)}, u32[]{:S(2)}) copy-start(f32[128]{0:T(128)S(1)} %get-tuple-element.31) | copy-start | bytes 1540
  177.5 157.0 %copy-start.67 = (f32[128]{0:T(128)}, f32[128]{0:T(128)S(1)}, u32[]{:S(2)}) copy-start(f32[128]{0:T(128)S(1)} %fusion.9) | copy-start | bytes 1540
  178.3 157.7 %copy-start.49 = (f32[128]{0:T(128)}, f32[128]{0:T(128)S(1)}, u32[]{:S(2)}) copy-start(f32[128]{0:T(128)S(1)} %get-tuple-element.29) | copy-start | bytes 1540
  178.7 157.3 %copy-start.64 = (f32[128]{0:T(128)}, f32[128]{0:T(128)S(1)}, u32[]{:S(2)}) copy-start(f32[128]{0:T(128)S(1)} %fusion.11) | copy-start | bytes 1540
  329.9 2.7 copy-start.6
  329.9 3.8 copy-start.78
  333.7 3.1 copy-start.36
  333.7 1.6 copy-start.3
  335.3 1.5 copy-start.38
  336.1 1.6 copy-start.44
  337.1 1.9 copy-start.42
  338.5 1.7 copy-start.21
  339.1 1.6 copy-start.56
  339.1 1.6 copy-start.71
  340.7 3.0 copy-start.34
  340.7 1.6 copy-start.9
  340.7 1.6 copy-start.59
  340.7 1.6 copy-start.74
  347.9 356.5 %reduce-scatter.3.cloned.1.call-start = ((), (), s32[]{:S(2)}) async-start(), calls=%async_computation.4 | async-start | bytes 8650752 | tf_op jit(solution)/shard_map/reduce_scatter | solution.py:167
  348.5 2.7 copy-start.10
  348.5 2.8 copy-start.61
  348.5 2.8 copy-start.76
  351.3 2.3 copy-start.79
  352.2 2.3 copy-start.7
  352.2 2.3 copy-start.57
  352.2 2.3 copy-start.72
  355.9 2.7 copy-start.13
  355.9 2.0 copy-start.4
  355.9 2.0 copy-start.54
  356.0 2.0 copy-start.69
  359.3 1.4 copy-start.15
  366.8 2.0 copy-start.14
  366.8 4.0 copy-start.16
  366.8 4.0 copy-start.12
  368.8 2.7 copy-start.18
  371.5 1.6 copy-start.29
  372.1 1.5 copy-start.27
  372.1 1.5 copy-start.37
  372.1 1.5 copy-start.39
  372.1 1.5 copy-start.41
  372.1 1.5 copy-start.43
  373.0 3.3 copy-start.22
  373.0 3.3 copy-start.33
  374.9 3.3 copy-start.81
  376.3 150.7 %copy-start.23 = (bf16[1,128,512]{2,1,0:T(8,128)(2,1)S(1)}, bf16[1,128,512]{2,1,0:T(8,128)(2,1)}, u32[]{:S(2)}) copy-start(bf16[1,128,512]{2,1,0:T(8,128)(2,1)} %param.13) | copy-start | bytes 393220
  378.1 328.8 %copy-start.46 = (f32[512]{0:T(512)S(1)}, f32[512]{0:T(512)}, u32[]{:S(2)}) copy-start(f32[512]{0:T(512)} %get-tuple-element.18) | copy-start | bytes 6148
  378.1 328.8 %copy-start.77 = (f32[512]{0:T(512)S(1)}, f32[512]{0:T(512)}, u32[]{:S(2)}) copy-start(f32[512]{0:T(512)} %fusion.14) | copy-start | bytes 6148
  707.0 118.6 %copy-start.1 = (bf16[512,1024]{1,0:T(8,128)(2,1)S(1)}, bf16[512,1024]{1,0:T(8,128)(2,1)}, u32[]{:S(2)}) copy-start(bf16[512,1024]{1,0:T(8,128)(2,1)} %param.20) | copy-start | bytes 3145732
  (23 other events, 22.6 us)
Sparse Core Ops, SparseCore 0:
  10.3 160.0 all-gather.2
  172.6 157.2 all-gather.4
  348.0 178.8 reduce-scatter.4
  529.2 175.1 reduce-scatter.2
where the time goes:
time: 833 us; the launch traced here: 832 us
  waiting for transfers between devices  630 us (76%)
  blocking collectives  114 us (14%)
  matrix products  41.7 us (5%)
  local copies, waits for them, and re-layouts  16 us (2%)
  between operations  14.7 us (2%)
  other arithmetic  14.5 us (2%)
    reduce_scatter x1, waiting for transfers between devices, local(): lax.psum_scatter(partial_keys.astype(jnp.float32), 'geom', scatter_dimens...  175 us
    all_gather x1, waiting for transfers between devices, local(): lax.all_gather(local_keys, 'geom', axis=0, tiled=True)  156 us
    all_gather x1, waiting for transfers between devices, local(): lax.all_gather(local_values, 'geom', axis=0, tiled=True)  151 us
    reduce_scatter x1, waiting for transfers between devices, local(): lax.psum_scatter(partial_values.astype(jnp.float32), 'geom', scatter_dime...  148 us
    psum x1, blocking collectives, local(): lax.psum((grad_query, grad_key, grad_value, grad_out, grad_up, grad_down,...  114 us
  transfers between devices with their start and end apart: 4, of which 4 were waited for; matrix products, arithmetic and copies ran while one was open for 5% of the time, Pallas kernels for 0%

commit v1 on v0

--- a/solution.py
+++ b/solution.py
@@ -141,13 +141,19 @@
     gain_attn,
     gain_mlp,
 ):
+
+    def region_recover(page, dev_axis):
+        return jnp.concatenate(
+            lax.all_to_all(jnp.stack(lax.axis_size(dev_axis) * [page], axis=0), dev_axis, 0, 0), 0
+        )
+
     local_feat = features[0]
     local_keys = jnp.dot(local_feat, w_key, preferred_element_type=jnp.float32).astype(jnp.bfloat16)
     local_values = jnp.dot(local_feat, w_value, preferred_element_type=jnp.float32).astype(
         jnp.bfloat16
     )
     key_rows, value_rows = (
-        lax.all_gather(local_keys, "geom", axis=0, tiled=True),
+        region_recover(local_keys, dev_axis="geom"),
         lax.all_gather(local_values, "geom", axis=0, tiled=True),
     )
     output, grads, partial_keys, partial_values = device_step(

time: 833 us -> 703 us (0.84)
  waiting for transfers between devices: 630 us -> 485 us
  starting transfers between devices: 0.34 us -> 9.92 us
    all_gather x1 -> x0, waiting for transfers between devices: 156 us -> none  [local(): lax.all_gather(local_keys, 'geom', axis=0, tiled=True)]
    all_to_all x0 -> x1, waiting for transfers between devices: none -> 64.3 us  [region_recover(): lax.all_to_all(jnp.stack(lax.axis_size(dev_axis) * [page], axis=0), dev_a...]
    all_gather x1, waiting for transfers between devices: 151 us -> 101 us  [local(): lax.all_gather(local_values, 'geom', axis=0, tiled=True)]
    all_to_all x0 -> x1, starting transfers between devices: none -> 9.62 us  [region_recover(): lax.all_to_all(jnp.stack(lax.axis_size(dev_axis) * [page], axis=0), dev_a...]
  transfers between devices with their start and end apart: 4 -> 4, of which waited for: 4 -> 4; matrix products, arithmetic and copies ran while one was open for 5% -> 6% of each run, Pallas kernels for 0% -> 0%
where the time goes in v1:
time: 703 us; the launch traced here: 702 us
  waiting for transfers between devices  485 us (69%)
  blocking collectives  115 us (16%)
  matrix products  47.1 us (7%)
  local copies, waits for them, and re-layouts  17.7 us (3%)
  between operations  14.7 us (2%)
  other arithmetic  12.7 us (2%)
  starting transfers between devices  9.92 us (1%)
    reduce_scatter x1, waiting for transfers between devices, local(): lax.psum_scatter(partial_keys.astype(jnp.float32), 'geom', scatter_dimens...  175 us
    reduce_scatter x1, waiting for transfers between devices, local(): lax.psum_scatter(partial_values.astype(jnp.float32), 'geom', scatter_dime...  144 us
    psum x1, blocking collectives, local(): lax.psum((grad_query, grad_key, grad_value, grad_out, grad_up, grad_down,...  115 us
    all_gather x1, waiting for transfers between devices, local(): lax.all_gather(local_values, 'geom', axis=0, tiled=True)  101 us
    all_to_all x1, waiting for transfers between devices, region_recover(): lax.all_to_all(jnp.stack(lax.axis_size(dev_axis) * [page], axis=0), dev_a...  64.3 us
    unnamed x164, local copies, waits for them, and re-layouts  15.2 us
    dot_general x12, matrix products, mult_nt(): lax.dot_general(left, right, (((1,), (1,)), ((), ())), preferred_element_...  14.9 us
  transfers between devices with their start and end apart: 4, of which 4 were waited for; matrix products, arithmetic and copies ran while one was open for 6% of the time, Pallas kernels for 0%

profile of v1, /device:TPU:0, one launch (start us, length us, event | category | flops | bytes accessed | tf_op | source)
XLA Modules:
  0.0 702.3 jit_solution(1977814720839745133)
XLA Ops:
  7.2 2.1 convolution_convert_fusion.9
  9.3 1.3 convolution_convert_fusion.10
  10.7 2.4 stack.2
  13.1 9.6 %all-to-all-start = ((bf16[32,128,512]{2,1,0:T(8,128)(2,1)}), bf16[32,128,512]{2,1,0:T(8,128)(2,1)}, u32[]{:S(2)}, u32[]{:S(2)}) async-start(bf16[32,128,512]{2,1,0:T(8,128)(2,1)} %stack.2), calls=%async_computation | async-start | bytes 8388608 | tf_op jit(solution)/shard_map/all_to_all | solution.py:147
  23.5 64.3 %all-to-all-done = bf16[32,128,512]{2,1,0:T(8,128)(2,1)} async-done(((bf16[32,128,512]{2,1,0:T(8,128)(2,1)}), bf16[32,128,512]{2,1,0:T(8,128)(2,1)}, u32[]{:S(2)}, u32[]{:S(2)}) %all-to-all-start) | async-done | bytes 4194336 | tf_op jit(solution)/shard_map/all_to_all | solution.py:147
  87.8 1.7 fusion.99
  89.6 1.4 copy-done.8
  90.9 0.4 fusion.5
  91.4 1.7 fusion.98
  93.2 1.3 copy-done.5
  94.4 0.4 fusion.7
  94.9 1.7 fusion.97
  96.7 0.4 fusion.9
  97.1 2.0 fusion.96
  99.2 0.4 fusion.11
  99.6 101.5 %all-gather.2.cloned.1.call-done = bf16[4096,512]{1,0:T(8,128)(2,1)} async-done(((bf16[128,512]{1,0:T(8,128)(2,1)}), bf16[4096,512]{1,0:T(8,128)(2,1)}) %all-gather.2.cloned.1.call-update) | async-done | bytes 4194320 | tf_op jit(solution)/shard_map/all_gather | solution.py:157
  201.1 2.7 convolution_convert_fusion.19
  203.8 1.0 copy-done.76
  204.9 0.7 convolution_convert_fusion.18
  205.6 0.8 copy-done.3
  206.5 0.7 convolution_convert_fusion.17
  207.3 0.7 convolution_convert_fusion.16
  209.3 0.8 copy-done.19
  210.1 0.6 fusion.12
  210.7 1.1 multiply_reduce_fusion.4
  212.4 0.6 convolution_convert_fusion.3
  213.1 0.6 convolution_convert_fusion.2
  213.7 0.6 convolution_convert_fusion.1
  214.4 0.6 convolution_convert_fusion
  215.0 3.6 maximum_convert_fusion.1
  219.3 2.7 multiply_reduce_fusion.3
  222.1 0.7 multiply_convert_fusion.3
  222.9 0.5 convolution_convert_fusion.7
  223.4 0.9 copy-done.77
  224.4 0.9 copy-done.7
  225.2 0.7 multiply_reduce_fusion.2
  225.9 0.7 multiply_convert_fusion.2
  226.7 0.5 convolution_convert_fusion.6
  227.2 1.5 copy-done.4
  228.6 0.7 multiply_reduce_fusion.1
  229.3 0.7 multiply_convert_fusion.1
  230.0 0.5 convolution_convert_fusion.5
  230.8 0.7 multiply_reduce_fusion
  231.4 0.7 multiply_convert_fusion
  232.2 1.0 copy-done.15
  233.1 0.5 convolution_convert_fusion.4
  233.6 3.9 maximum_convert_fusion
  237.5 1.9 convolution_convert_fusion.15
  239.5 1.9 convolution_convert_fusion.14
  241.4 1.8 convolution_convert_fusion.13
  243.2 1.8 convolution_convert_fusion.12
  245.1 0.9 fusion.14
  246.0 0.5 fusion.86
  246.6 1.3 fusion.79
  247.9 1.4 fusion.78
  249.3 1.8 fusion.55
  251.1 1.0 fusion.15
  252.1 144.0 %reduce-scatter.5.cloned.1.call-done = f32[128,512]{1,0:T(8,128)} async-done(((f32[4096,512]{1,0:T(8,128)}), f32[128,512]{1,0:T(8,128)}) %reduce-scatter.5.cloned.1.call-update) | async-done | bytes 262160 | tf_op jit(solution)/shard_map/reduce_scatter | solution.py:174
  396.1 2.6 convolution_bitcast_fusion
  398.7 175.4 %reduce-scatter.3.cloned.1.call-done = f32[128,512]{1,0:T(8,128)} async-done(((f32[4096,512]{1,0:T(8,128)}), f32[128,512]{1,0:T(8,128)}) %reduce-scatter.3.cloned.1.call-update) | async-done | bytes 262160 | tf_op jit(solution)/shard_map/reduce_scatter | solution.py:173
  574.1 2.5 convolution_bitcast_fusion.1
  576.6 115.0 %all-reduce.2 = (bf16[512,512]{1,0:T(8,128)(2,1)}, bf16[512,512]{0,1:T(8,128)(2,1)}, bf16[512,512]{0,1:T(8,128)(2,1)}, bf16[512,512]{1,0:T(8,128)(2,1)}, bf16[51...) all-reduce(f32[512,512]{1,0:T(8,128)} %fusion.78, ...), channel_id=1, replica_groups=mesh['room'=4,'geom'=32] {'room','geom'}, use_global_device_ids=true, to_apply=%region_18.19 | all-reduce | flops 2098176 | bytes 12589056 | tf_op jit(solution)/shard_map/psum | solution.py:194
  691.7 2.0 copy.21
  693.7 2.0 copy.22
  (174 shorter events, 4.0 us)
Async XLA Ops:
  7.2 201.7 %copy-start = (bf16[512,1024]{1,0:T(8,128)(2,1)S(1)}, bf16[512,1024]{1,0:T(8,128)(2,1)}, u32[]{:S(2)}) copy-start(bf16[512,1024]{1,0:T(8,128)(2,1)} %param.20) | copy-start | bytes 3145732
  7.2 193.9 %all-gather.2.cloned.1.call-start = ((), (), s32[]{:S(2)}) async-start(), calls=%async_computation.3 | async-start | bytes 4325376 | tf_op jit(solution)/shard_map/all_gather | solution.py:157
  13.1 9.7 %copy-start.17 = (bf16[1,128,512]{2,1,0:T(8,128)(2,1)S(1)}, bf16[1,128,512]{2,1,0:T(8,128)(2,1)}, u32[]{:S(2)}) copy-start(bf16[1,128,512]{2,1,0:T(8,128)(2,1)} %param.12) | copy-start | bytes 393220
  13.1 10.0 %copy-start.80 = (s32[1,1,32]{2,1,0:T(1,128)S(1)}, s32[1,1,32]{2,1,0:T(1,128)}, u32[]{:S(2)}) copy-start(s32[1,1,32]{2,1,0:T(1,128)} %param.14) | copy-start | bytes 388
  13.1 10.1 %copy-start.28 = (bf16[512,512]{1,0:T(8,128)(2,1)S(1)}, bf16[512,512]{1,0:T(8,128)(2,1)}, u32[]{:S(2)}) copy-start(bf16[512,512]{1,0:T(8,128)(2,1)} %param.16) | copy-start | bytes 1572868
  13.1 10.1 %copy-start.43 = (f32[512]{0:T(512)S(1)}, f32[512]{0:T(512)}, u32[]{:S(2)}) copy-start(f32[512]{0:T(512)} %param.22) | copy-start | bytes 6148
  13.1 74.7 %all-to-all-start = ((bf16[32,128,512]{2,1,0:T(8,128)(2,1)}), bf16[32,128,512]{2,1,0:T(8,128)(2,1)}, u32[]{:S(2)}, u32[]{:S(2)}) async-start(bf16[32,128,512]{2,1,0:T(8,128)(2,1)} %stack.2), calls=%async_computation | async-start | bytes 8388608 | tf_op jit(solution)/shard_map/all_to_all | solution.py:147
  22.7 373.4 %reduce-scatter.5.cloned.1.call-start = ((), (), s32[]{:S(2)}) async-start(), calls=%async_computation.5 | async-start | bytes 8650752 | tf_op jit(solution)/shard_map/reduce_scatter | solution.py:174
  22.9 68.5 %copy-start.45 = (f32[128]{0:T(128)}, f32[128]{0:T(128)S(1)}, u32[]{:S(2)}) copy-start(f32[128]{0:T(128)S(1)} %broadcast_multiply_fusion.3) | copy-start | bytes 1540
  23.1 68.2 %copy-start.60 = (f32[128]{0:T(128)}, f32[128]{0:T(128)S(1)}, u32[]{:S(2)}) copy-start(f32[128]{0:T(128)S(1)} %add_rsqrt_fusion.1) | copy-start | bytes 1540
  23.5 73.6 %copy-start.22 = (bf16[128,512]{1,0:T(8,128)(2,1)}, bf16[128,512]{1,0:T(8,128)(2,1)S(1)}, u32[]{:S(2)}) copy-start(bf16[128,512]{1,0:T(8,128)(2,1)S(1)} %convolution_convert_fusion.11) | copy-start | bytes 393220
  89.6 111.5 %copy-start.56 = (f32[128]{0:T(128)}, f32[128]{0:T(128)S(1)}, u32[]{:S(2)}) copy-start(f32[128]{0:T(128)S(1)} %get-tuple-element.35) | copy-start | bytes 1540
  91.4 109.7 %copy-start.71 = (f32[128]{0:T(128)}, f32[128]{0:T(128)S(1)}, u32[]{:S(2)}) copy-start(f32[128]{0:T(128)S(1)} %fusion.5) | copy-start | bytes 1540
  93.1 110.7 %copy-start.53 = (f32[128]{0:T(128)}, f32[128]{0:T(128)S(1)}, u32[]{:S(2)}) copy-start(f32[128]{0:T(128)S(1)} %get-tuple-element.33) | copy-start | bytes 1540
  94.9 108.9 %copy-start.68 = (f32[128]{0:T(128)}, f32[128]{0:T(128)S(1)}, u32[]{:S(2)}) copy-start(f32[128]{0:T(128)S(1)} %fusion.7) | copy-start | bytes 1540
  96.6 2.5 copy-start.2
  96.6 109.0 %copy-start.50 = (f32[128]{0:T(128)}, f32[128]{0:T(128)S(1)}, u32[]{:S(2)}) copy-start(f32[128]{0:T(128)S(1)} %get-tuple-element.31) | copy-start | bytes 1540
  97.1 108.5 %copy-start.65 = (f32[128]{0:T(128)}, f32[128]{0:T(128)S(1)}, u32[]{:S(2)}) copy-start(f32[128]{0:T(128)S(1)} %fusion.9) | copy-start | bytes 1540
  99.1 108.1 %copy-start.47 = (f32[128]{0:T(128)}, f32[128]{0:T(128)S(1)}, u32[]{:S(2)}) copy-start(f32[128]{0:T(128)S(1)} %get-tuple-element.29) | copy-start | bytes 1540
  99.6 107.6 %copy-start.62 = (f32[128]{0:T(128)}, f32[128]{0:T(128)S(1)}, u32[]{:S(2)}) copy-start(f32[128]{0:T(128)S(1)} %fusion.11) | copy-start | bytes 1540
  201.1 2.7 copy-start.6
  201.1 3.8 copy-start.76
  204.9 3.1 copy-start.34
  204.9 1.6 copy-start.3
  206.5 1.5 copy-start.36
  207.3 1.7 copy-start.42
  208.3 1.8 copy-start.30
  208.3 1.8 copy-start.78
  210.7 1.7 copy-start.9
  210.7 1.7 copy-start.57
  210.7 1.7 copy-start.72
  212.4 2.0 copy-start.32
  218.6 355.5 %reduce-scatter.3.cloned.1.call-start = ((), (), s32[]{:S(2)}) async-start(), calls=%async_computation.4 | async-start | bytes 8650752 | tf_op jit(solution)/shard_map/reduce_scatter | solution.py:173
  219.3 2.7 copy-start.10
  219.3 2.7 copy-start.59
  219.3 2.7 copy-start.74
  222.0 2.3 copy-start.77
  222.9 2.3 copy-start.7
  222.9 2.3 copy-start.55
  222.9 2.3 copy-start.70
  226.6 2.7 copy-start.11
  226.6 2.0 copy-start.4
  226.6 2.0 copy-start.52
  226.7 2.0 copy-start.67
  230.0 1.4 copy-start.13
  237.5 1.9 copy-start.12
  237.5 3.8 copy-start.14
  239.5 3.8 copy-start.16
  241.3 3.7 copy-start.29
  241.4 3.7 copy-start.46
  241.4 3.7 copy-start.61
  243.2 2.8 copy-start.27
  245.1 1.5 copy-start.25
  245.1 1.5 copy-start.35
  245.1 1.5 copy-start.37
  245.1 1.5 copy-start.39
  245.1 1.5 copy-start.41
  246.0 3.3 copy-start.20
  246.0 3.3 copy-start.31
  247.9 3.3 copy-start.79
  249.3 146.8 %copy-start.21 = (bf16[1,128,512]{2,1,0:T(8,128)(2,1)S(1)}, bf16[1,128,512]{2,1,0:T(8,128)(2,1)}, u32[]{:S(2)}) copy-start(bf16[1,128,512]{2,1,0:T(8,128)(2,1)} %param.13) | copy-start | bytes 393220
  251.1 325.5 %copy-start.44 = (f32[512]{0:T(512)S(1)}, f32[512]{0:T(512)}, u32[]{:S(2)}) copy-start(f32[512]{0:T(512)} %get-tuple-element.18) | copy-start | bytes 6148
  251.1 325.5 %copy-start.75 = (f32[512]{0:T(512)S(1)}, f32[512]{0:T(512)}, u32[]{:S(2)}) copy-start(f32[512]{0:T(512)} %fusion.14) | copy-start | bytes 6148
  576.6 119.1 %copy-start.1 = (bf16[512,1024]{1,0:T(8,128)(2,1)S(1)}, bf16[512,1024]{1,0:T(8,128)(2,1)}, u32[]{:S(2)}) copy-start(bf16[512,1024]{1,0:T(8,128)(2,1)} %param.20) | copy-start | bytes 3145732
  (21 other events, 18.2 us)
Sparse Core Ops, SparseCore 0:
  10.2 190.7 all-gather.1
  218.7 177.3 reduce-scatter.4
  398.5 175.5 reduce-scatter.2
